TPU v7x, 32 devices: a whole 2x2x4 slice. The times are simulated.
32 devices in a mesh: grp: 2 (over x), tok: 4 (over z), head: 4 (over y, core).
Axes of the slice: x: 2, y: 2, z: 4, core: 2. Of those that a mesh axis runs over, the one named last changes fastest.
Arguments:
- views: bfloat16 [2, 2, 768, 1024], P('grp', None, 'tok'), may hold values from -6 to 6
- q_weight: bfloat16 [1024, 1024], P(None, 'head'), may hold values from -0.1875 to 0.1875
- k_weight: bfloat16 [1024, 1024], P(None, 'head'), may hold values from -0.1875 to 0.1875
- v_weight: bfloat16 [1024, 1024], P(None, 'head'), may hold values from -0.1875 to 0.1875
- rate_weight: bfloat16 [1024, 4], P(None, 'head'), may hold values from -0.1875 to 0.1875
- fast_in: float32 [4, 256, 1024], P('head', None, 'tok'), may hold values from -0.375 to 0.375
- fast_out: float32 [4, 512, 256], P('head', None, 'tok'), may hold values from -0.25 to 0.25
- out_gain: float32 [1024], P('head'), may hold values from 0.1 to 1.9
Outputs:
- rendered: bfloat16 [2, 2, 768, 1024], P('grp', None, 'tok', 'head')
All inputs are finite; a program needn't handle non-finite values.
Results may differ from a plain program's by a relative error of at most 0.013.
Values may be sent and summed in bfloat16 or wider, within the bound.
A program may use at most 64 MiB of HBM per device.

v0:
```python
import functools
import math

import jax
import jax.numpy as jnp
from jax import lax
from jax.experimental import pallas as pl
from jax.experimental.pallas import tpu as pltpu
from jax.sharding import PartitionSpec as P

norm_eps = 1e-06
out_eps = 1e-05
step_coef = 0.3
momentum_keep = 0.5


def spread(value, axis, source):
    kept = jnp.where(lax.axis_index(axis) == source, value, 0).astype(value.dtype)
    return lax.psum(kept, axis)


def rms_scale(values):
    return values * lax.rsqrt(jnp.mean(values * values, axis=-1, keepdims=True) + norm_eps)


def contract_rows(left, right):
    return lax.dot_general(
        left, right, (((0,), (0,)), ((), ())), preferred_element_type=jnp.float32
    )


def contract_cols(left, right):
    return lax.dot_general(
        left, right, (((1,), (1,)), ((), ())), preferred_element_type=jnp.float32
    )


def fast_apply(queries, copy_in, copy_out):
    hidden_units = copy_out.shape[0]
    pre_act = jnp.dot(queries, copy_in, preferred_element_type=jnp.float32)
    gate = pre_act[:, :hidden_units]
    upper = pre_act[:, hidden_units:]
    hidden = (gate * jax.nn.sigmoid(gate) * upper).astype(jnp.bfloat16)
    return jnp.dot(hidden, copy_out, preferred_element_type=jnp.float32)


def by_collectives(views, q_weight, k_weight, v_weight, rate_weight, fast_in, fast_out, out_gain):
    tok_count = lax.axis_size("tok")
    is_input = lax.axis_index("grp") == 0
    spans = views.shape[1]
    head_size = fast_in.shape[1]
    hidden_units = fast_out.shape[1]
    step_size = step_coef / math.sqrt(views.shape[2] * tok_count)
    width_all = head_size * lax.axis_size("head")
    whole_in, whole_out = (
        lax.all_gather(fast_in, "tok", axis=2, tiled=True),
        lax.all_gather(fast_out, "tok", axis=2, tiled=True),
    )
    whole_in = whole_in[0]
    whole_out = whole_out[0]
    copy_in = whole_in.astype(jnp.bfloat16)
    copy_out = whole_out.astype(jnp.bfloat16)
    state_in = fast_in[0]
    state_out = fast_out[0]
    base_in = jnp.mean(state_in * state_in, axis=0, keepdims=True)
    base_out = jnp.mean(state_out * state_out, axis=0, keepdims=True)
    moment_in = jnp.zeros_like(state_in)
    moment_out = jnp.zeros_like(state_out)

    def input_grads(inputs, given_in, given_out):
        keyed = rms_scale(jnp.dot(inputs, k_weight, preferred_element_type=jnp.float32)).astype(
            jnp.bfloat16
        )
        valued = jnp.dot(inputs, v_weight, preferred_element_type=jnp.float32)
        rates = jax.nn.softplus(jnp.dot(inputs, rate_weight, preferred_element_type=jnp.float32))
        upstream = (-(step_size * rates) * valued).astype(jnp.bfloat16)
        pre_act = jnp.dot(keyed, given_in, preferred_element_type=jnp.float32)
        gate = pre_act[:, :hidden_units]
        upper = pre_act[:, hidden_units:]
        sigma = jax.nn.sigmoid(gate)
        active = gate * sigma
        hidden = (active * upper).astype(jnp.bfloat16)
        grad_out = contract_rows(hidden, upstream)
        back = contract_cols(upstream, given_out)
        back_pre = jnp.concatenate(
            [back * upper * sigma * (1.0 + gate * (1.0 - sigma)), back * active], axis=1
        ).astype(jnp.bfloat16)
        grad_in = contract_rows(keyed, back_pre)
        return (grad_in, grad_out)

    def novel_grads(inputs, given_in, given_out):
        return (
            jnp.zeros((head_size, 2 * hidden_units), jnp.float32),
            jnp.zeros((hidden_units, head_size), jnp.float32),
        )

    outputs = []
    for span in range(spans):
        inputs = views[0, span]
        queries = rms_scale(jnp.dot(inputs, q_weight, preferred_element_type=jnp.float32)).astype(
            jnp.bfloat16
        )
        grads = lax.cond(is_input, input_grads, novel_grads, inputs, copy_in, copy_out)
        grad_in, grad_out = lax.psum_scatter(grads, "tok", scatter_dimension=1, tiled=True)
        moment_in = momentum_keep * moment_in + grad_in
        moment_out = momentum_keep * moment_out + grad_out
        trial_in = state_in - moment_in
        trial_out = state_out - moment_out
        mean_in = jnp.mean(trial_in * trial_in, axis=0, keepdims=True)
        mean_out = jnp.mean(trial_out * trial_out, axis=0, keepdims=True)
        state_in = trial_in * jnp.sqrt(base_in) * lax.rsqrt(mean_in + norm_eps)
        state_out = trial_out * jnp.sqrt(base_out) * lax.rsqrt(mean_out + norm_eps)
        part_in = state_in.astype(jnp.bfloat16)
        part_out = state_out.astype(jnp.bfloat16)
        copy_in, copy_out = (
            lax.all_gather(part_in, "tok", axis=1, tiled=True),
            lax.all_gather(part_out, "tok", axis=1, tiled=True),
        )
        copy_in, copy_out = (spread(copy_in, "grp", 0), spread(copy_out, "grp", 0))
        produced = fast_apply(queries, copy_in, copy_out)
        squares = lax.psum(jnp.sum(produced * produced, axis=1), "head")
        normed = produced * lax.rsqrt(squares / width_all + out_eps)[:, None] * out_gain
        outputs.append(normed.astype(jnp.bfloat16))
    return jnp.stack(outputs)[None]


def fused_kernel(
    tok_count, grp_count, head_count,
    views_ref, q_ref, k_ref, v_ref, rate_ref, in_ref, out_ref, gain_ref,
    res_ref,
    pieces, packed, queries, keys, ups, moment_in, moment_out, state_in, state_out, copy_in, copy_out,
    base_in, base_out, produced, squares,
    local_sem,
    first_send, first_recv, z_send, z_recv, x_send, x_recv, y_send, y_recv,
    c1_send, c1_recv, c2_send, c2_recv, wz_send, wz_recv, wx_send, wx_recv, sq_send, sq_recv,
):
    tok, grp, head = lax.axis_index("tok"), lax.axis_index("grp"), lax.axis_index("head")
    spans, rows, width = views_ref.shape[1:]
    piece = pieces.shape[-1]
    head_size, block_in = in_ref.shape[1:]
    block_out, hidden_units = out_ref.shape[1:]
    fold = packed.shape[-1] - block_in
    folds = hidden_units // fold
    half = head_size // grp_count
    step_size = step_coef / math.sqrt(rows * tok_count)
    other_grp = {"grp": 1 - grp}
    far_bit = head_count // 2
    far_head = jnp.where(head < far_bit, head + far_bit, head - far_bit)
    flip = 1 - 2 * lax.rem(head, 2)
    near_head = head + flip
    far = {"head": far_head}
    near = {"head": near_head}

    def shard(step):
        return lax.rem(tok - step + tok_count, tok_count)

    def peer(step):
        return {"tok": lax.rem(tok + step, tok_count)}

    def remote(src, dst, send, recv, target):
        return pltpu.make_async_remote_copy(
            src_ref=src, dst_ref=dst, send_sem=send, recv_sem=recv,
            device_id=target, device_id_type=pl.DeviceIdType.MESH,
        )

    def view_piece(span, part):
        start = pl.multiple_of((head * grp_count + part) * piece, piece)
        return views_ref.at[0, span, :, pl.ds(start, piece)]

    def same(ref, send, recv, target):
        return remote(ref, ref, send, recv, target)

    own = [
        pltpu.make_async_copy(view_piece(s, 0), pieces.at[s, tok, head, 0], local_sem.at[s])
        for s in range(spans)
    ]
    first = [
        remote(view_piece(s, 1), pieces.at[s, tok, head, 1], first_send.at[s], first_recv.at[s], other_grp)
        for s in range(spans)
    ]
    along_z = [
        [
            same(pieces.at[s, tok, head, grp], z_send.at[s, d], z_recv.at[s, d], peer(d + 1))
            for d in range(tok_count - 1)
        ]
        for s in range(spans)
    ]
    along_x = [
        [
            same(pieces.at[s, shard(d), head, grp], x_send.at[s, d], x_recv.at[s, d], other_grp)
            for d in range(tok_count)
        ]
        for s in range(spans)
    ]
    y_own, y_other = [
        [
            [
                same(pieces.at[s, shard(d), head, part], y_send.at[s, d, i], y_recv.at[s, d, i], far)
                for d in range(tok_count)
            ]
            for s in range(spans)
        ]
        for i, part in enumerate((grp, 1 - grp))
    ]
    core_own = [
        [
            same(pieces.at[s, shard(d), head], c1_send.at[s, d], c1_recv.at[s, d], near)
            for d in range(tok_count)
        ]
        for s in range(spans)
    ]
    core_far = [
        [
            same(pieces.at[s, shard(d), far_head], c2_send.at[s, d], c2_recv.at[s, d], near)
            for d in range(tok_count)
        ]
        for s in range(spans)
    ]
    my_half = pl.ds(pl.multiple_of(grp * half, half), half)
    fast_z = [
        same(packed.at[tok, my_half], wz_send.at[d], wz_recv.at[d], peer(d + 1))
        for d in range(tok_count - 1)
    ]
    fast_x = [
        same(packed.at[shard(d + 1), my_half], wx_send.at[d], wx_recv.at[d], other_grp)
        for d in range(tok_count - 1)
    ]
    square = [
        [
            same(squares.at[s, head], sq_send.at[s, d], sq_recv.at[s, d],
                 {"head": lax.rem(head + d + 1, head_count)})
            for d in range(head_count - 1)
        ]
        for s in range(spans)
    ]

    barrier = pltpu.get_barrier_semaphore()
    partners = [peer(d + 1) for d in range(tok_count - 1)] + [other_grp]
    partners += [{"head": lax.rem(head + d + 1, head_count)} for d in range(head_count - 1)]
    for target in partners:
        pl.semaphore_signal(barrier, inc=1, device_id=target, device_id_type=pl.DeviceIdType.MESH)

    @pl.when(grp == 0)
    def _():
        for copy in own:
            copy.start()

    packed[tok, :, :block_in] = in_ref[0].astype(jnp.bfloat16)
    for f in range(folds):
        packed[tok, f * block_out:(f + 1) * block_out, block_in:] = out_ref[
            0, :, f * fold:(f + 1) * fold
        ].astype(jnp.bfloat16)
    pl.semaphore_wait(barrier, len(partners))

    @pl.when(grp == 0)
    def _():
        for s in range(spans):
            first[s].start()
        for copy in own:
            copy.wait()
        for copy in along_z[0]:
            copy.start()

    @pl.when(grp == 1)
    def _():
        first[0].wait_recv()
        for copy in along_z[0]:
            copy.start()

    along_x[0][0].start()
    y_own[0][0].start()

    @pl.when(grp == 1)
    def _():
        for s in range(1, spans):
            first[s].wait_recv()

    for s in range(1, spans):
        along_x[s][0].start()
        y_own[s][0].start()
        for copy in along_z[s]:
            copy.start()
    for copy in fast_z:
        copy.start()

    def project_queries(span):
        queries[span] = rms_scale(
            jnp.dot(views_ref[0, span], q_ref[...], preferred_element_type=jnp.float32)
        ).astype(jnp.bfloat16)

    def project(span, t):
        inputs = jnp.concatenate(
            [pieces[span, t, h, g] for h in range(head_count) for g in range(grp_count)], axis=1
        )
        keys[span, t] = rms_scale(
            jnp.dot(inputs, k_ref[...], preferred_element_type=jnp.float32)
        ).astype(jnp.bfloat16)
        valued = jnp.dot(inputs, v_ref[...], preferred_element_type=jnp.float32)
        raw = contract_cols(inputs, jnp.broadcast_to(rate_ref[...], (8, width)))[:, :1]
        rates = jnp.maximum(raw, 0.0) + jnp.log1p(jnp.exp(-jnp.abs(raw)))
        ups[span, t] = (-(step_size * rates) * valued).astype(jnp.bfloat16)

    def forward(span, step):
        if 1 <= step - 1 < tok_count:
            along_x[span][step - 1].wait_recv()
            y_other[span][step - 1].start()
            core_own[span][step - 1].start()
        if 0 <= step - 2 < tok_count:
            y_own[span][step - 2].wait_recv()
            y_other[span][step - 2].wait_recv()
            core_far[span][step - 2].start()
        if 0 <= step - 3 < tok_count:
            core_own[span][step - 3].wait_recv()
            core_far[span][step - 3].wait_recv()
            project(span, shard(step - 3))

    def pass_on(span, step):
        along_z[span][step - 1].wait_recv()
        along_x[span][step].start()
        y_own[span][step].start()

    last_step = tok_count + 2
    for s in range(spans):
        along_x[s][0].wait_recv()
        y_other[s][0].start()
        core_own[s][0].start()
    project_queries(0)
    for step in range(1, last_step + 1):
        if step < tok_count:
            pass_on(0, step)
        forward(0, step)
        for s in range(1, spans):
            if 0 <= step - tok_count < tok_count - 1:
                pass_on(s, step - tok_count + 1)
    for d in range(tok_count - 1):
        fast_z[d].wait_recv()
        fast_x[d].start()
    for s in range(1, spans):
        for step in range(1, tok_count + 2):
            forward(s, step)
    for s in range(1, spans):
        project_queries(s)
    for d in range(tok_count - 1):
        fast_x[d].wait_recv()

    for t in range(tok_count):
        cols = slice(t * block_in, (t + 1) * block_in)
        given = packed[t, :, :block_in]
        wide = given.astype(jnp.float32)
        copy_in[:, cols] = given
        state_in[:, cols] = wide
        base_in[:, cols] = jnp.sqrt(jnp.mean(wide * wide, axis=0, keepdims=True))
        for f in range(folds):
            part = slice(f * fold, (f + 1) * fold)
            turned = slice(t * block_out, (t + 1) * block_out)
            given = packed[t, f * block_out:(f + 1) * block_out, block_in:]
            copy_out[turned, part] = given
            state_out[turned, part] = given.astype(jnp.float32)
    base_out[...] = jnp.sqrt(jnp.mean(state_out[...] * state_out[...], axis=1, keepdims=True))
    moment_in[...] = jnp.zeros_like(moment_in)
    moment_out[...] = jnp.zeros_like(moment_out)

    def add_grads(span, t):
        keyed, upstream = keys[span, t], ups[span, t]
        gate = jnp.dot(keyed, copy_in[:, :hidden_units], preferred_element_type=jnp.float32)
        upper = jnp.dot(keyed, copy_in[:, hidden_units:], preferred_element_type=jnp.float32)
        sigma = jax.nn.sigmoid(gate)
        active = gate * sigma
        hidden = (active * upper).astype(jnp.bfloat16)
        moment_out[...] += contract_rows(upstream, hidden)
        back = jnp.dot(upstream, copy_out[...], preferred_element_type=jnp.float32)
        back_gate = (back * upper * sigma * (1.0 + gate * (1.0 - sigma))).astype(jnp.bfloat16)
        back_upper = (back * active).astype(jnp.bfloat16)
        moment_in[:, :hidden_units] += contract_rows(keyed, back_gate)
        moment_in[:, hidden_units:] += contract_rows(keyed, back_upper)

    def renormalize(state, moment, base, axis):
        trial = state - moment
        mean = jnp.mean(trial * trial, axis=axis, keepdims=True)
        return trial * base * lax.rsqrt(mean + norm_eps)

    for s in range(spans):
        for d in range(tok_count):
            add_grads(s, d)
            if s + 1 < spans:
                if tok_count + 2 + d <= last_step:
                    forward(s + 1, tok_count + 2 + d)
        for t in range(tok_count):
            cols = slice(t * block_in, (t + 1) * block_in)
            fresh = renormalize(state_in[:, cols], moment_in[:, cols], base_in[:, cols], 0)
            copy_in[:, cols] = fresh.astype(jnp.bfloat16)
            if s + 1 < spans:
                state_in[:, cols] = fresh
                moment_in[:, cols] *= momentum_keep
            turned = slice(t * block_out, (t + 1) * block_out)
            fresh = renormalize(state_out[turned], moment_out[turned], base_out[turned], 1)
            copy_out[turned] = fresh.astype(jnp.bfloat16)
            if s + 1 < spans:
                state_out[turned] = fresh
                moment_out[turned] *= momentum_keep
        pre_act = jnp.dot(queries[s], copy_in[...], preferred_element_type=jnp.float32)
        gate = pre_act[:, :hidden_units]
        hidden = (gate * jax.nn.sigmoid(gate) * pre_act[:, hidden_units:]).astype(jnp.bfloat16)
        made = contract_cols(hidden, copy_out[...])
        produced[s] = made
        sums = jnp.sum(made * made, axis=1, keepdims=True)
        squares[s, head] = jnp.transpose(jnp.broadcast_to(sums, (rows, 128)))[:8]
        for copy in square[s]:
            copy.start()

    for s in range(spans):
        for copy in square[s]:
            copy.wait_recv()
        total = squares[s, 0]
        for h in range(1, head_count):
            total = total + squares[s, h]
        scale = lax.rsqrt(total / (head_size * head_count) + out_eps)
        column = jnp.transpose(jnp.concatenate([scale] * 16, axis=0))[:, :1]
        res_ref[0, s] = (produced[s] * column * gain_ref[...]).astype(jnp.bfloat16)

    @pl.when(grp == 0)
    def _():
        for copy in first:
            copy.wait_send()

    for group in (along_z, along_x, y_own, y_other, core_own, core_far, square):
        for copies in group:
            for copy in copies:
                copy.wait_send()
    for copy in fast_z + fast_x:
        copy.wait_send()


def by_kernel(sizes, views, q_weight, k_weight, v_weight, rate_weight, fast_in, fast_out, out_gain):
    tok_count, grp_count, head_count = sizes
    _, spans, rows, width = views.shape
    _, head_size, block_in = fast_in.shape
    _, hidden_units, block_out = fast_out.shape
    piece = width // (grp_count * head_count)
    fold = hidden_units * block_out // head_size
    dma = pltpu.SemaphoreType.DMA
    vmem = pltpu.VMEM
    pair = [dma((spans, tok_count))] * 2
    return pl.pallas_call(
        functools.partial(fused_kernel, tok_count, grp_count, head_count),
        out_shape=jax.ShapeDtypeStruct((1, spans, rows, head_size), jnp.bfloat16),
        in_specs=[pl.BlockSpec(memory_space=pltpu.VMEM)] * 8,
        out_specs=pl.BlockSpec(memory_space=pltpu.VMEM),
        scratch_shapes=[
            vmem((spans, tok_count, head_count, grp_count, rows, piece), jnp.bfloat16),
            vmem((tok_count, head_size, block_in + fold), jnp.bfloat16),
            vmem((spans, rows, head_size), jnp.bfloat16),
            vmem((spans, tok_count, rows, head_size), jnp.bfloat16),
            vmem((spans, tok_count, rows, head_size), jnp.bfloat16),
            vmem((head_size, 2 * hidden_units), jnp.float32),
            vmem((head_size, hidden_units), jnp.float32),
            vmem((head_size, 2 * hidden_units), jnp.float32),
            vmem((head_size, hidden_units), jnp.float32),
            vmem((head_size, 2 * hidden_units), jnp.bfloat16),
            vmem((head_size, hidden_units), jnp.bfloat16),
            vmem((1, 2 * hidden_units), jnp.float32),
            vmem((head_size, 1), jnp.float32),
            vmem((spans, rows, head_size), jnp.float32),
            vmem((spans, head_count, 8, rows), jnp.float32),
            dma((spans,)),
            *[dma((spans,))] * 2,
            *[dma((spans, tok_count - 1))] * 2,
            *pair, *[dma((spans, tok_count, 2))] * 2, *pair, *pair,
            *[dma((tok_count - 1,))] * 4,
            *[dma((spans, head_count - 1))] * 2,
        ],
        compiler_params=pltpu.CompilerParams(collective_id=0, has_side_effects=True),
        name="fused_layer",
    )(
        views, q_weight, k_weight, v_weight, rate_weight.T, fast_in,
        jnp.swapaxes(fast_out, 1, 2), out_gain.reshape(1, -1),
    )


def local(sizes, views, *rest):
    tok_count, grp_count, head_count = sizes
    fast_in, fast_out = rest[4], rest[5]
    head_size, hidden_units = fast_in.shape[1], fast_out.shape[1]
    piece = views.shape[3] // (grp_count * head_count)
    few = tok_count * views.shape[2] <= 4 * head_size
    fits = (
        tok_count > 1 and grp_count == 2 and head_count == 4 and piece % 128 == 0
        and fast_in.shape[2] % 128 == 0 and views.shape[2] % 16 == 0 and head_size % fast_out.shape[2] == 0
        and fast_out.shape[2] * hidden_units % (128 * head_size) == 0 and fast_out.shape[2] % 16 == 0
    )
    if few and fits:
        return by_kernel(sizes, views, *rest)
    return by_collectives(views, *rest)


def solution(mesh):
    sizes = (mesh.shape["tok"], mesh.shape["grp"], mesh.shape["head"])
    placed = (
        P("grp", None, "tok", None),
        P(None, "head"),
        P(None, "head"),
        P(None, "head"),
        P(None, "head"),
        P("head", None, "tok"),
        P("head", None, "tok"),
        P("head"),
    )
    return jax.shard_map(
        functools.partial(local, sizes), mesh=mesh, in_specs=placed, out_specs=P("grp", None, "tok", "head"), check_vma=False
    )
```

profile of v0, /device:TPU:0, one launch (start us, length us, event | category | flops | bytes accessed | tf_op | source)
XLA Modules:
  0.0 51.0 jit_solution(18057276949575135498)
XLA Ops:
  0.0 49.4 %fused_layer.1 = bf16[1,2,192,256]{3,2,1,0:T(8,128)(2,1)} custom-call(bf16[1,2,192,1024]{3,2,1,0:T(8,128)(2,1)} %views_ref.1, bf16[1024,256]{1,0:T(8,128)(2,1)} %q_ref.1, bf16[1024,256]{1,0:T(8,128)(2,1)} %k_ref.1, bf16[1024,256]{1,0:T(8,128)(2,1)} %v_ref.1, bf16[1,1024]{1,0:T(2,128)(2,1)} %bitcast.4, f32[1,256,256]{2,1,0:T(8,128)} %in_ref.1, ...), custom_call_target="tpu_custom_call" | custom-call | tf_op jit(solution)/shard_map/fused_layer/pallas_call | solution.py:444
  49.4 1.6 %copy.10 = bf16[1,2,192,256]{3,2,1,0:T(8,128)(2,1)} copy(bf16[1,2,192,256]{3,2,1,0:T(8,128)(2,1)} %fused_layer.1) | data formatting | bytes 393216
where the time goes:
time: 51.1 us; the launch traced here: 51 us
  Pallas kernels  49.4 us (97%)
  local copies, waits for them, and re-layouts  1.62 us (3%)
    pallas_call x1, Pallas kernels, by_kernel(): pl.pallas_call(functools.partial(fused_kernel, tok_count, grp_count, head...  49.4 us
    unnamed x1, local copies, waits for them, and re-layouts  1.62 us

commit v1 on v0

--- a/solution.py
+++ b/solution.py
@@ -126,36 +126,53 @@
 
 def fused_kernel(
     tok_count, grp_count, head_count,
-    views_ref, q_ref, k_ref, v_ref, rate_ref, in_ref, out_ref, gain_ref,
+    views_ref, q_hbm, k_hbm, v_hbm, rate_hbm, in_hbm, out_hbm, gain_hbm,
     res_ref,
+    local_views, q_ref, k_ref, v_ref, rate_ref, in_ref, out_ref, gain_ref,
     pieces, packed, queries, keys, ups, moment_in, moment_out, state_in, state_out, copy_in, copy_out,
     base_in, base_out, produced, squares,
-    local_sem,
-    first_send, first_recv, z_send, z_recv, x_send, x_recv, y_send, y_recv,
+    load_sem, own_sem,
+    z_send, z_recv, x_send, x_recv, y_send, y_recv,
     c1_send, c1_recv, c2_send, c2_recv, wz_send, wz_recv, wx_send, wx_recv, sq_send, sq_recv,
 ):
     tok, grp, head = lax.axis_index("tok"), lax.axis_index("grp"), lax.axis_index("head")
     spans, rows, width = views_ref.shape[1:]
     piece = pieces.shape[-1]
-    head_size, block_in = in_ref.shape[1:]
-    block_out, hidden_units = out_ref.shape[1:]
+    head_size, block_in = in_ref.shape
+    block_out, hidden_units = out_ref.shape
     fold = packed.shape[-1] - block_in
     folds = hidden_units // fold
-    half = head_size // grp_count
+    strip = head_size // 4
+    strips = [slice(p * strip, (p + 1) * strip) for p in range(4)]
     step_size = step_coef / math.sqrt(rows * tok_count)
-    other_grp = {"grp": 1 - grp}
+    last_tok = tok_count - 1
     far_bit = head_count // 2
     far_head = jnp.where(head < far_bit, head + far_bit, head - far_bit)
-    flip = 1 - 2 * lax.rem(head, 2)
-    near_head = head + flip
+    near_head = head + 1 - 2 * lax.rem(head, 2)
+    other = {"grp": 1 - grp}
     far = {"head": far_head}
     near = {"head": near_head}
-
-    def shard(step):
-        return lax.rem(tok - step + tok_count, tok_count)
-
-    def peer(step):
-        return {"tok": lax.rem(tok + step, tok_count)}
+    above = {"tok": jnp.minimum(tok + 1, last_tok)}
+    below = {"tok": jnp.maximum(tok - 1, 0)}
+    skip = {"tok": jnp.where(tok * 2 < tok_count, tok + 2, tok - 2)}
+    outer = {"tok": jnp.where(tok * 2 < tok_count, jnp.maximum(tok - 1, 0), jnp.minimum(tok + 1, last_tok))}
+    has_above, has_below = tok < last_tok, tok > 0
+    is_input, is_novel = grp == 0, grp == 1
+
+    low = tok * 2 < tok_count
+    inner = jnp.where(low, tok, last_tok - tok)
+    flip = jnp.where(low, 1, -1)
+
+    def shard(place):
+        if place == 0:
+            return tok
+        step = (place + 1) // 2 * (1 if place % 2 else -1)
+        return jnp.where(
+            place <= 2 * inner, tok + flip * step, jnp.where(low, place, last_tok - place)
+        )
+
+    shards = [shard(i) for i in range(tok_count)]
+    sent = []
 
     def remote(src, dst, send, recv, target):
         return pltpu.make_async_remote_copy(
@@ -163,187 +180,198 @@
             device_id=target, device_id_type=pl.DeviceIdType.MESH,
         )
 
-    def view_piece(span, part):
-        start = pl.multiple_of((head * grp_count + part) * piece, piece)
-        return views_ref.at[0, span, :, pl.ds(start, piece)]
-
     def same(ref, send, recv, target):
         return remote(ref, ref, send, recv, target)
 
+    def send(copy, cond=None):
+        sent.append((copy, cond))
+        if cond is None:
+            copy.start()
+        else:
+            pl.when(cond)(copy.start)
+
+    def view_piece(span, h, part):
+        start = pl.multiple_of((h * grp_count + part) * piece, piece)
+        return views_ref.at[0, span, :, pl.ds(start, piece)]
+
+    def block(span, i, h, part):
+        return pieces.at[span, shards[i], h, part]
+
+    loads = [
+        pltpu.make_async_copy(src, dst, load_sem.at[n])
+        for n, (src, dst) in enumerate([
+            (in_hbm.at[0], in_ref), (out_hbm.at[0], out_ref), (views_ref.at[0], local_views), (q_hbm, q_ref),
+            (k_hbm, k_ref), (v_hbm, v_ref), (rate_hbm, rate_ref), (gain_hbm, gain_ref),
+        ])
+    ]
     own = [
-        pltpu.make_async_copy(view_piece(s, 0), pieces.at[s, tok, head, 0], local_sem.at[s])
-        for s in range(spans)
-    ]
-    first = [
-        remote(view_piece(s, 1), pieces.at[s, tok, head, 1], first_send.at[s], first_recv.at[s], other_grp)
-        for s in range(spans)
-    ]
-    along_z = [
         [
-            same(pieces.at[s, tok, head, grp], z_send.at[s, d], z_recv.at[s, d], peer(d + 1))
-            for d in range(tok_count - 1)
+            pltpu.make_async_copy(view_piece(s, h, g), pieces.at[s, tok, h, g], own_sem.at[s, h, g])
+            for h in range(head_count) for g in range(grp_count)
         ]
         for s in range(spans)
     ]
-    along_x = [
-        [
-            same(pieces.at[s, shard(d), head, grp], x_send.at[s, d], x_recv.at[s, d], other_grp)
-            for d in range(tok_count)
-        ]
-        for s in range(spans)
-    ]
-    y_own, y_other = [
-        [
-            [
-                same(pieces.at[s, shard(d), head, part], y_send.at[s, d, i], y_recv.at[s, d, i], far)
-                for d in range(tok_count)
-            ]
-            for s in range(spans)
-        ]
-        for i, part in enumerate((grp, 1 - grp))
-    ]
-    core_own = [
-        [
-            same(pieces.at[s, shard(d), head], c1_send.at[s, d], c1_recv.at[s, d], near)
-            for d in range(tok_count)
-        ]
-        for s in range(spans)
-    ]
-    core_far = [
-        [
-            same(pieces.at[s, shard(d), far_head], c2_send.at[s, d], c2_recv.at[s, d], near)
-            for d in range(tok_count)
-        ]
-        for s in range(spans)
-    ]
-    my_half = pl.ds(pl.multiple_of(grp * half, half), half)
-    fast_z = [
-        same(packed.at[tok, my_half], wz_send.at[d], wz_recv.at[d], peer(d + 1))
-        for d in range(tok_count - 1)
-    ]
-    fast_x = [
-        same(packed.at[shard(d + 1), my_half], wx_send.at[d], wx_recv.at[d], other_grp)
-        for d in range(tok_count - 1)
-    ]
-    square = [
-        [
-            same(squares.at[s, head], sq_send.at[s, d], sq_recv.at[s, d],
-                 {"head": lax.rem(head + d + 1, head_count)})
-            for d in range(head_count - 1)
-        ]
-        for s in range(spans)
-    ]
 
     barrier = pltpu.get_barrier_semaphore()
-    partners = [peer(d + 1) for d in range(tok_count - 1)] + [other_grp]
-    partners += [{"head": lax.rem(head + d + 1, head_count)} for d in range(head_count - 1)]
-    for target in partners:
+
+    def greet(target):
         pl.semaphore_signal(barrier, inc=1, device_id=target, device_id_type=pl.DeviceIdType.MESH)
 
-    @pl.when(grp == 0)
+    greet(other)
+    greet(skip)
+    greet(far)
+    greet(near)
+    pl.when(has_above)(lambda: greet(above))
+    pl.when(has_below)(lambda: greet(below))
+    for copy in loads:
+        copy.start()
+
+    @pl.when(is_input)
     def _():
-        for copy in own:
-            copy.start()
-
-    packed[tok, :, :block_in] = in_ref[0].astype(jnp.bfloat16)
+        for copies in own:
+            for copy in copies:
+                copy.start()
+
+    loads[0].wait()
+    loads[1].wait()
+    packed[tok, :, :block_in] = in_ref[...].astype(jnp.bfloat16)
     for f in range(folds):
         packed[tok, f * block_out:(f + 1) * block_out, block_in:] = out_ref[
-            0, :, f * fold:(f + 1) * fold
+            :, f * fold:(f + 1) * fold
         ].astype(jnp.bfloat16)
-    pl.semaphore_wait(barrier, len(partners))
-
-    @pl.when(grp == 0)
-    def _():
-        for s in range(spans):
-            first[s].start()
-        for copy in own:
-            copy.wait()
-        for copy in along_z[0]:
-            copy.start()
-
-    @pl.when(grp == 1)
-    def _():
-        first[0].wait_recv()
-        for copy in along_z[0]:
-            copy.start()
-
-    along_x[0][0].start()
-    y_own[0][0].start()
-
-    @pl.when(grp == 1)
-    def _():
-        for s in range(1, spans):
-            first[s].wait_recv()
-
-    for s in range(1, spans):
-        along_x[s][0].start()
-        y_own[s][0].start()
-        for copy in along_z[s]:
-            copy.start()
-    for copy in fast_z:
-        copy.start()
+    pl.semaphore_wait(barrier, 4 + jnp.where(has_above, 1, 0) + jnp.where(has_below, 1, 0))
+
+    parts = range(grp_count)
+    quarters = range(len(strips))
+    relays = has_above & has_below
+    sides = (is_input, is_novel)
+
+    def carrier(s, part):
+        return ((0, 0), (0, 1))[s][part]
+
+    def weight_carrier(q):
+        return (0, 1, 1, 1)[q]
+
+    def z_copy(s, i, part, way, target, fresh=False):
+        src = view_piece(s, head, part) if fresh else block(s, i, head, part)
+        return remote(
+            src, block(s, i, head, part), z_send.at[s, i, part, way], z_recv.at[s, shards[i], part], target
+        )
+
+    def w_copy(i, q, way, target):
+        return same(packed.at[shards[i], strips[q]], wz_send.at[i, q, way], wz_recv.at[shards[i], q], target)
+
+    def x_copy(s, i, part, fresh=False):
+        src = view_piece(s, head, part) if fresh else block(s, i, head, part)
+        return remote(src, block(s, i, head, part), x_send.at[s, i, part], x_recv.at[s, i, part], other)
+
+    def y_copy(s, i, part):
+        return same(block(s, i, head, part), y_send.at[s, i, part], y_recv.at[s, i, part], far)
+
+    def c_copy(s, i, n, part):
+        h, snd, rcv = ((head, c1_send, c1_recv), (far_head, c2_send, c2_recv))[n]
+        return same(block(s, i, h, part), snd.at[s, i, part], rcv.at[s, i, part], near)
+
+    def x_weights(i, q):
+        return same(packed.at[shards[i], strips[q]], wx_send.at[i, q], wx_recv.at[i, q], other)
+
+    def fan(side, copy):
+        for way, (target, cond) in enumerate(((above, has_above), (below, has_below), (skip, None))):
+            send(copy(way, target), side if cond is None else cond & side)
+
+    def own_views(s, part):
+        fresh = carrier(s, part) == 0
+        fan(sides[carrier(s, part)], lambda way, target: z_copy(s, 0, part, way, target, fresh))
+
+    def own_weights(q):
+        fan(sides[weight_carrier(q)], lambda way, target: w_copy(0, q, way, target))
+
+    def own_across(s, part):
+        send(x_copy(s, 0, part, True), is_input)
+
+    def spread_on(s, i, part, cond):
+        send(y_copy(s, i, part), cond)
+        send(c_copy(s, i, 0, part), cond)
+
+    def start_own(s, part):
+        if carrier(s, part) == 0:
+            own_views(s, part)
+
+    def pass_z(s, i, part):
+        side = sides[carrier(s, part)]
+        pl.when(side)(z_copy(s, i, part, 0, above).wait_recv)
+        if i == last_tok:
+            send(z_copy(s, i, part, 0, outer), relays & side)
+        send(x_copy(s, i, part), side)
+        spread_on(s, i, part, side)
+
+    def pass_x(s, i, part):
+        side = is_novel if i == 0 else sides[1 - carrier(s, part)]
+        pl.when(side)(x_copy(s, i, part).wait_recv)
+        if i == 0 and carrier(s, part) == 1:
+            own_views(s, part)
+        spread_on(s, i, part, side)
+
+    def pass_y(s, i, part):
+        cond = is_novel if i == 0 else None
+        if cond is None:
+            y_copy(s, i, part).wait_recv()
+        else:
+            pl.when(cond)(y_copy(s, i, part).wait_recv)
+        send(c_copy(s, i, 1, part), cond)
+
+    def take(s, i):
+        def waits():
+            for n in range(2):
+                for part in parts:
+                    c_copy(s, i, n, part).wait_recv()
+        if i == 0:
+            pl.when(is_novel)(waits)
+
+            @pl.when(is_input)
+            def _():
+                for copy in own[s]:
+                    copy.wait()
+        else:
+            waits()
+        project(s, i)
+
+    def pass_weights(i, q):
+        side = sides[weight_carrier(q)]
+        pl.when(side)(w_copy(i, q, 0, above).wait_recv)
+        if i == last_tok:
+            send(w_copy(i, q, 0, outer), relays & side)
+        send(x_weights(i, q), side)
+
+    def unpack_all():
+        for i in range(1, tok_count):
+            for q in quarters:
+                pl.when(sides[1 - weight_carrier(q)])(x_weights(i, q).wait_recv)
+        for t in range(tok_count):
+            unpack(t)
+        base_out[...] = jnp.sqrt(jnp.mean(state_out[...] * state_out[...], axis=1, keepdims=True))
+        moment_in[...] = jnp.zeros_like(moment_in)
+        moment_out[...] = jnp.zeros_like(moment_out)
 
     def project_queries(span):
         queries[span] = rms_scale(
-            jnp.dot(views_ref[0, span], q_ref[...], preferred_element_type=jnp.float32)
+            jnp.dot(local_views[span], q_ref[...], preferred_element_type=jnp.float32)
         ).astype(jnp.bfloat16)
 
-    def project(span, t):
+    def project(span, i):
+        t = shards[i]
         inputs = jnp.concatenate(
             [pieces[span, t, h, g] for h in range(head_count) for g in range(grp_count)], axis=1
         )
-        keys[span, t] = rms_scale(
+        keys[span, i] = rms_scale(
             jnp.dot(inputs, k_ref[...], preferred_element_type=jnp.float32)
         ).astype(jnp.bfloat16)
         valued = jnp.dot(inputs, v_ref[...], preferred_element_type=jnp.float32)
         raw = contract_cols(inputs, jnp.broadcast_to(rate_ref[...], (8, width)))[:, :1]
         rates = jnp.maximum(raw, 0.0) + jnp.log1p(jnp.exp(-jnp.abs(raw)))
-        ups[span, t] = (-(step_size * rates) * valued).astype(jnp.bfloat16)
-
-    def forward(span, step):
-        if 1 <= step - 1 < tok_count:
-            along_x[span][step - 1].wait_recv()
-            y_other[span][step - 1].start()
-            core_own[span][step - 1].start()
-        if 0 <= step - 2 < tok_count:
-            y_own[span][step - 2].wait_recv()
-            y_other[span][step - 2].wait_recv()
-            core_far[span][step - 2].start()
-        if 0 <= step - 3 < tok_count:
-            core_own[span][step - 3].wait_recv()
-            core_far[span][step - 3].wait_recv()
-            project(span, shard(step - 3))
-
-    def pass_on(span, step):
-        along_z[span][step - 1].wait_recv()
-        along_x[span][step].start()
-        y_own[span][step].start()
-
-    last_step = tok_count + 2
-    for s in range(spans):
-        along_x[s][0].wait_recv()
-        y_other[s][0].start()
-        core_own[s][0].start()
-    project_queries(0)
-    for step in range(1, last_step + 1):
-        if step < tok_count:
-            pass_on(0, step)
-        forward(0, step)
-        for s in range(1, spans):
-            if 0 <= step - tok_count < tok_count - 1:
-                pass_on(s, step - tok_count + 1)
-    for d in range(tok_count - 1):
-        fast_z[d].wait_recv()
-        fast_x[d].start()
-    for s in range(1, spans):
-        for step in range(1, tok_count + 2):
-            forward(s, step)
-    for s in range(1, spans):
-        project_queries(s)
-    for d in range(tok_count - 1):
-        fast_x[d].wait_recv()
-
-    for t in range(tok_count):
+        ups[span, i] = (-(step_size * rates) * valued).astype(jnp.bfloat16)
+
+    def unpack(t):
         cols = slice(t * block_in, (t + 1) * block_in)
         given = packed[t, :, :block_in]
         wide = given.astype(jnp.float32)
@@ -356,9 +384,6 @@
             given = packed[t, f * block_out:(f + 1) * block_out, block_in:]
             copy_out[turned, part] = given
             state_out[turned, part] = given.astype(jnp.float32)
-    base_out[...] = jnp.sqrt(jnp.mean(state_out[...] * state_out[...], axis=1, keepdims=True))
-    moment_in[...] = jnp.zeros_like(moment_in)
-    moment_out[...] = jnp.zeros_like(moment_out)
 
     def add_grads(span, t):
         keyed, upstream = keys[span, t], ups[span, t]
@@ -379,12 +404,7 @@
         mean = jnp.mean(trial * trial, axis=axis, keepdims=True)
         return trial * base * lax.rsqrt(mean + norm_eps)
 
-    for s in range(spans):
-        for d in range(tok_count):
-            add_grads(s, d)
-            if s + 1 < spans:
-                if tok_count + 2 + d <= last_step:
-                    forward(s + 1, tok_count + 2 + d)
+    def update(s):
         for t in range(tok_count):
             cols = slice(t * block_in, (t + 1) * block_in)
             fresh = renormalize(state_in[:, cols], moment_in[:, cols], base_in[:, cols], 0)
@@ -398,6 +418,17 @@
             if s + 1 < spans:
                 state_out[turned] = fresh
                 moment_out[turned] *= momentum_keep
+
+    square = [
+        [
+            same(squares.at[s, head], sq_send.at[s, d], sq_recv.at[s, d],
+                 {"head": lax.rem(head + d + 1, head_count)})
+            for d in range(head_count - 1)
+        ]
+        for s in range(spans)
+    ]
+
+    def apply(s):
         pre_act = jnp.dot(queries[s], copy_in[...], preferred_element_type=jnp.float32)
         gate = pre_act[:, :hidden_units]
         hidden = (gate * jax.nn.sigmoid(gate) * pre_act[:, hidden_units:]).astype(jnp.bfloat16)
@@ -406,9 +437,9 @@
         sums = jnp.sum(made * made, axis=1, keepdims=True)
         squares[s, head] = jnp.transpose(jnp.broadcast_to(sums, (rows, 128)))[:8]
         for copy in square[s]:
-            copy.start()
-
-    for s in range(spans):
+            send(copy)
+
+    def finish(s):
         for copy in square[s]:
             copy.wait_recv()
         total = squares[s, 0]
@@ -418,17 +449,106 @@
         column = jnp.transpose(jnp.concatenate([scale] * 16, axis=0))[:, :1]
         res_ref[0, s] = (produced[s] * column * gain_ref[...]).astype(jnp.bfloat16)
 
-    @pl.when(grp == 0)
-    def _():
-        for copy in first:
+    own_across(1, 1)
+    start_own(0, 0)
+    own_across(0, 1)
+    own_weights(1)
+    pass_x(1, 0, 1)
+    pass_x(0, 0, 1)
+    own_across(0, 0)
+    pass_x(0, 0, 0)
+    pass_x(1, 0, 0)
+    own_across(1, 0)
+    start_own(0, 1)
+    pass_z(0, 2, 0)
+    pass_weights(1, 1)
+    pass_z(0, 1, 0)
+    pass_z(0, 1, 1)
+    own_weights(3)
+    pass_weights(1, 3)
+    for copy in loads[2:]:
+        copy.wait()
+    project_queries(0)
+    own_weights(2)
+    pass_z(1, 2, 1)
+    start_own(1, 0)
+    pass_z(0, 2, 1)
+    pass_weights(2, 1)
+    pass_x(0, 1, 0)
+    pass_x(0, 1, 1)
+    pass_z(0, 3, 0)
+    pass_x(0, 2, 0)
+    pass_z(1, 1, 0)
+    own_weights(0)
+    pass_z(1, 2, 0)
+    pass_weights(2, 3)
+    pass_x(0, 2, 1)
+    pass_z(1, 1, 1)
+    pass_weights(3, 1)
+    pass_z(0, 3, 1)
+    pass_z(1, 3, 0)
+    pass_weights(2, 2)
+    pass_x(1, 2, 1)
+    pass_x(0, 3, 0)
+    pass_y(0, 1, 0)
+    project_queries(1)
+    pass_weights(3, 3)
+    pass_x(0, 3, 1)
+    pass_weights(2, 0)
+    pass_weights(1, 2)
+    pass_y(0, 0, 1)
+    pass_y(0, 0, 0)
+    pass_weights(1, 0)
+    pass_weights(3, 0)
+    pass_weights(3, 2)
+    pass_y(1, 0, 1)
+    pass_y(0, 2, 1)
+    pass_x(1, 1, 0)
+    take(0, 0)
+    pass_y(0, 1, 1)
+    pass_x(1, 2, 0)
+    pass_z(1, 3, 1)
+    pass_x(1, 3, 0)
+    pass_y(1, 0, 0)
+    pass_x(1, 1, 1)
+    pass_y(0, 2, 0)
+    pass_y(0, 3, 1)
+    take(0, 1)
+    pass_y(1, 2, 1)
+    take(1, 0)
+    pass_y(0, 3, 0)
+    take(0, 2)
+    unpack_all()
+    add_grads(0, 0)
+    pass_y(1, 1, 0)
+    pass_y(1, 2, 0)
+    take(0, 3)
+    pass_y(1, 1, 1)
+    pass_x(1, 3, 1)
+    add_grads(0, 1)
+    add_grads(0, 3)
+    add_grads(0, 2)
+    update(0)
+    start_own(1, 1)
+    take(1, 1)
+    take(1, 2)
+    apply(0)
+    pass_y(1, 3, 0)
+    pass_y(1, 3, 1)
+    add_grads(1, 2)
+    add_grads(1, 1)
+    add_grads(1, 0)
+    take(1, 3)
+    add_grads(1, 3)
+    update(1)
+    apply(1)
+    finish(0)
+    finish(1)
+    for copy, cond in sent:
+        if cond is None:
             copy.wait_send()
-
-    for group in (along_z, along_x, y_own, y_other, core_own, core_far, square):
-        for copies in group:
-            for copy in copies:
-                copy.wait_send()
-    for copy in fast_z + fast_x:
-        copy.wait_send()
+        else:
+            pl.when(cond)(copy.wait_send)
 
 
 def by_kernel(sizes, views, q_weight, k_weight, v_weight, rate_weight, fast_in, fast_out, out_gain):
@@ -440,13 +560,18 @@
     fold = hidden_units * block_out // head_size
     dma = pltpu.SemaphoreType.DMA
     vmem = pltpu.VMEM
-    pair = [dma((spans, tok_count))] * 2
     return pl.pallas_call(
         functools.partial(fused_kernel, tok_count, grp_count, head_count),
         out_shape=jax.ShapeDtypeStruct((1, spans, rows, head_size), jnp.bfloat16),
-        in_specs=[pl.BlockSpec(memory_space=pltpu.VMEM)] * 8,
+        in_specs=[pl.BlockSpec(memory_space=pl.ANY)] * 8,
         out_specs=pl.BlockSpec(memory_space=pltpu.VMEM),
         scratch_shapes=[
+            vmem((spans, rows, width), jnp.bfloat16),
+            *[vmem((width, head_size), jnp.bfloat16)] * 3,
+            vmem((1, width), jnp.bfloat16),
+            vmem((head_size, block_in), jnp.float32),
+            vmem((block_out, hidden_units), jnp.float32),
+            vmem((1, head_size), jnp.float32),
             vmem((spans, tok_count, head_count, grp_count, rows, piece), jnp.bfloat16),
             vmem((tok_count, head_size, block_in + fold), jnp.bfloat16),
             vmem((spans, rows, head_size), jnp.bfloat16),
@@ -462,11 +587,11 @@
             vmem((head_size, 1), jnp.float32),
             vmem((spans, rows, head_size), jnp.float32),
             vmem((spans, head_count, 8, rows), jnp.float32),
-            dma((spans,)),
-            *[dma((spans,))] * 2,
-            *[dma((spans, tok_count - 1))] * 2,
-            *pair, *[dma((spans, tok_count, 2))] * 2, *pair, *pair,
-            *[dma((tok_count - 1,))] * 4,
+            dma((8,)), dma((spans, head_count, grp_count)),
+            dma((spans, tok_count, grp_count, 3)), dma((spans, tok_count, grp_count)),
+            *[dma((spans, tok_count, grp_count))] * 8,
+            dma((tok_count, 4, 3)), dma((tok_count, 4)),
+            *[dma((tok_count, 4))] * 2,
             *[dma((spans, head_count - 1))] * 2,
         ],
         compiler_params=pltpu.CompilerParams(collective_id=0, has_side_effects=True),
@@ -484,7 +609,7 @@
     piece = views.shape[3] // (grp_count * head_count)
     few = tok_count * views.shape[2] <= 4 * head_size
     fits = (
-        tok_count > 1 and grp_count == 2 and head_count == 4 and piece % 128 == 0
+        tok_count == 4 and grp_count == 2 and head_count == 4 and piece % 128 == 0
         and fast_in.shape[2] % 128 == 0 and views.shape[2] % 16 == 0 and head_size % fast_out.shape[2] == 0
         and fast_out.shape[2] * hidden_units % (128 * head_size) == 0 and fast_out.shape[2] % 16 == 0
     )

time: 51.1 us -> 48.2 us (0.943)
  Pallas kernels: 49.4 us -> 46.4 us
    pallas_call x1, Pallas kernels: 49.4 us -> 46.4 us  [by_kernel(): pl.pallas_call(functools.partial(fused_kernel, tok_count, grp_count, head...]
where the time goes in v1:
time: 48.2 us; the launch traced here: 48.1 us
  Pallas kernels  46.4 us (96%)
  local copies, waits for them, and re-layouts  1.62 us (3%)
    pallas_call x1, Pallas kernels, by_kernel(): pl.pallas_call(functools.partial(fused_kernel, tok_count, grp_count, head...  46.4 us
    unnamed x1, local copies, waits for them, and re-layouts  1.62 us

profile of v1, /device:TPU:0, one launch (start us, length us, event | category | flops | bytes accessed | tf_op | source)
XLA Modules:
  0.0 48.1 jit_solution(17743336128265565696)
XLA Ops:
  0.0 46.4 %fused_layer.1 = bf16[1,2,192,256]{3,2,1,0:T(8,128)(2,1)} custom-call(bf16[1,2,192,1024]{3,2,1,0:T(8,128)(2,1)} %views_ref.1, bf16[1024,256]{1,0:T(8,128)(2,1)} %q_hbm.1, bf16[1024,256]{1,0:T(8,128)(2,1)} %k_hbm.1, bf16[1024,256]{1,0:T(8,128)(2,1)} %v_hbm.1, bf16[1,1024]{1,0:T(2,128)(2,1)} %bitcast.4, f32[1,256,256]{2,1,0:T(8,128)} %in_hbm.1, ...), custom_call_target="tpu_custom_call" | custom-call | tf_op jit(solution)/shard_map/fused_layer/pallas_call | solution.py:563
  46.5 1.6 %copy.10 = bf16[1,2,192,256]{3,2,1,0:T(8,128)(2,1)} copy(bf16[1,2,192,256]{3,2,1,0:T(8,128)(2,1)} %fused_layer.1) | data formatting | bytes 393216

commit v2 on v1

--- a/solution.py
+++ b/solution.py
@@ -347,11 +347,8 @@
         for i in range(1, tok_count):
             for q in quarters:
                 pl.when(sides[1 - weight_carrier(q)])(x_weights(i, q).wait_recv)
-        for t in range(tok_count):
-            unpack(t)
+            unpack(shards[i])
         base_out[...] = jnp.sqrt(jnp.mean(state_out[...] * state_out[...], axis=1, keepdims=True))
-        moment_in[...] = jnp.zeros_like(moment_in)
-        moment_out[...] = jnp.zeros_like(moment_out)
 
     def project_queries(span):
         queries[span] = rms_scale(
@@ -363,16 +360,17 @@
         inputs = jnp.concatenate(
             [pieces[span, t, h, g] for h in range(head_count) for g in range(grp_count)], axis=1
         )
-        keys[span, i] = rms_scale(
+        lines = slice(i * rows, (i + 1) * rows)
+        keys[span, lines] = rms_scale(
             jnp.dot(inputs, k_ref[...], preferred_element_type=jnp.float32)
         ).astype(jnp.bfloat16)
         valued = jnp.dot(inputs, v_ref[...], preferred_element_type=jnp.float32)
         raw = contract_cols(inputs, jnp.broadcast_to(rate_ref[...], (8, width)))[:, :1]
         rates = jnp.maximum(raw, 0.0) + jnp.log1p(jnp.exp(-jnp.abs(raw)))
-        ups[span, i] = (-(step_size * rates) * valued).astype(jnp.bfloat16)
+        ups[span, lines] = (-(step_size * rates) * valued).astype(jnp.bfloat16)
 
     def unpack(t):
-        cols = slice(t * block_in, (t + 1) * block_in)
+        cols = pl.ds(pl.multiple_of(t * block_in, block_in), block_in)
         given = packed[t, :, :block_in]
         wide = given.astype(jnp.float32)
         copy_in[:, cols] = given
@@ -380,24 +378,36 @@
         base_in[:, cols] = jnp.sqrt(jnp.mean(wide * wide, axis=0, keepdims=True))
         for f in range(folds):
             part = slice(f * fold, (f + 1) * fold)
-            turned = slice(t * block_out, (t + 1) * block_out)
+            turned = pl.ds(pl.multiple_of(t * block_out, block_out), block_out)
             given = packed[t, f * block_out:(f + 1) * block_out, block_in:]
             copy_out[turned, part] = given
             state_out[turned, part] = given.astype(jnp.float32)
 
-    def add_grads(span, t):
-        keyed, upstream = keys[span, t], ups[span, t]
-        gate = jnp.dot(keyed, copy_in[:, :hidden_units], preferred_element_type=jnp.float32)
-        upper = jnp.dot(keyed, copy_in[:, hidden_units:], preferred_element_type=jnp.float32)
+    def add_grads(span, start, count):
+        lines = slice(start * rows, (start + count) * rows)
+        keyed, upstream = keys[span, lines], ups[span, lines]
+
+        def gather(moment, cols, left, right):
+            grads = contract_rows(left, right)
+            if span == 0 and start == 0:
+                moment[:, cols] = grads
+            elif start == 0:
+                moment[:, cols] = momentum_keep * moment[:, cols] + grads
+            else:
+                moment[:, cols] += grads
+
+        first, second = slice(0, hidden_units), slice(hidden_units, 2 * hidden_units)
+        gate = jnp.dot(keyed, copy_in[:, first], preferred_element_type=jnp.float32)
+        upper = jnp.dot(keyed, copy_in[:, second], preferred_element_type=jnp.float32)
         sigma = jax.nn.sigmoid(gate)
         active = gate * sigma
         hidden = (active * upper).astype(jnp.bfloat16)
-        moment_out[...] += contract_rows(upstream, hidden)
+        gather(moment_out, first, upstream, hidden)
         back = jnp.dot(upstream, copy_out[...], preferred_element_type=jnp.float32)
         back_gate = (back * upper * sigma * (1.0 + gate * (1.0 - sigma))).astype(jnp.bfloat16)
         back_upper = (back * active).astype(jnp.bfloat16)
-        moment_in[:, :hidden_units] += contract_rows(keyed, back_gate)
-        moment_in[:, hidden_units:] += contract_rows(keyed, back_upper)
+        gather(moment_in, first, keyed, back_gate)
+        gather(moment_in, second, keyed, back_upper)
 
     def renormalize(state, moment, base, axis):
         trial = state - moment
@@ -411,13 +421,11 @@
             copy_in[:, cols] = fresh.astype(jnp.bfloat16)
             if s + 1 < spans:
                 state_in[:, cols] = fresh
-                moment_in[:, cols] *= momentum_keep
             turned = slice(t * block_out, (t + 1) * block_out)
             fresh = renormalize(state_out[turned], moment_out[turned], base_out[turned], 1)
             copy_out[turned] = fresh.astype(jnp.bfloat16)
             if s + 1 < spans:
                 state_out[turned] = fresh
-                moment_out[turned] *= momentum_keep
 
     square = [
         [
@@ -468,6 +476,7 @@
     pass_weights(1, 3)
     for copy in loads[2:]:
         copy.wait()
+    unpack(tok)
     project_queries(0)
     own_weights(2)
     pass_z(1, 2, 1)
@@ -519,15 +528,12 @@
     pass_y(0, 3, 0)
     take(0, 2)
     unpack_all()
-    add_grads(0, 0)
     pass_y(1, 1, 0)
     pass_y(1, 2, 0)
     take(0, 3)
     pass_y(1, 1, 1)
     pass_x(1, 3, 1)
-    add_grads(0, 1)
-    add_grads(0, 3)
-    add_grads(0, 2)
+    add_grads(0, 0, 4)
     update(0)
     start_own(1, 1)
     take(1, 1)
@@ -535,11 +541,9 @@
     apply(0)
     pass_y(1, 3, 0)
     pass_y(1, 3, 1)
-    add_grads(1, 2)
-    add_grads(1, 1)
-    add_grads(1, 0)
+    add_grads(1, 0, 3)
     take(1, 3)
-    add_grads(1, 3)
+    add_grads(1, 3, 1)
     update(1)
     apply(1)
     finish(0)
@@ -575,8 +579,8 @@
             vmem((spans, tok_count, head_count, grp_count, rows, piece), jnp.bfloat16),
             vmem((tok_count, head_size, block_in + fold), jnp.bfloat16),
             vmem((spans, rows, head_size), jnp.bfloat16),
-            vmem((spans, tok_count, rows, head_size), jnp.bfloat16),
-            vmem((spans, tok_count, rows, head_size), jnp.bfloat16),
+            vmem((spans, tok_count * rows, head_size), jnp.bfloat16),
+            vmem((spans, tok_count * rows, head_size), jnp.bfloat16),
             vmem((head_size, 2 * hidden_units), jnp.float32),
             vmem((head_size, hidden_units), jnp.float32),
             vmem((head_size, 2 * hidden_units), jnp.float32),

time: 48.2 us -> 47.1 us (0.977)
  Pallas kernels: 46.4 us -> 45.4 us
    pallas_call x1, Pallas kernels: 46.4 us -> 45.4 us  [by_kernel(): pl.pallas_call(functools.partial(fused_kernel, tok_count, grp_count, head...]
where the time goes in v2:
time: 47.1 us; the launch traced here: 47 us
  Pallas kernels  45.4 us (96%)
  local copies, waits for them, and re-layouts  1.62 us (3%)
    pallas_call x1, Pallas kernels, by_kernel(): pl.pallas_call(functools.partial(fused_kernel, tok_count, grp_count, head...  45.4 us
    unnamed x1, local copies, waits for them, and re-layouts  1.62 us

profile of v2, /device:TPU:0, one launch (start us, length us, event | category | flops | bytes accessed | tf_op | source)
XLA Modules:
  0.0 47.0 jit_solution(10879149467385812291)
XLA Ops:
  0.0 45.4 %fused_layer.1 = bf16[1,2,192,256]{3,2,1,0:T(8,128)(2,1)} custom-call(bf16[1,2,192,1024]{3,2,1,0:T(8,128)(2,1)} %views_ref.1, bf16[1024,256]{1,0:T(8,128)(2,1)} %q_hbm.1, bf16[1024,256]{1,0:T(8,128)(2,1)} %k_hbm.1, bf16[1024,256]{1,0:T(8,128)(2,1)} %v_hbm.1, bf16[1,1024]{1,0:T(2,128)(2,1)} %bitcast.4, f32[1,256,256]{2,1,0:T(8,128)} %in_hbm.1, ...), custom_call_target="tpu_custom_call" | custom-call | tf_op jit(solution)/shard_map/fused_layer/pallas_call | solution.py:567
  45.4 1.6 %copy.10 = bf16[1,2,192,256]{3,2,1,0:T(8,128)(2,1)} copy(bf16[1,2,192,256]{3,2,1,0:T(8,128)(2,1)} %fused_layer.1) | data formatting | bytes 393216
